TPU v7x, 256 devices: a whole 4x4x8 slice. The times are simulated.
256 devices in a mesh: aux: 2 (over core), row: 8 (over z), col: 16 (over x, y).
Axes of the slice: x: 4, y: 4, z: 8, core: 2. Of those that a mesh axis runs over, the one named last changes fastest.
Arguments:
- coulomb: bfloat16 [64, 2048, 2048], P('aux', 'row', 'col'), may hold values from -6 to 6
- occupied: bfloat16 [2048, 2048], P('row'), may hold values from -0.125 to 0.125
- virtual: bfloat16 [2048, 2048], P('row'), may hold values from -0.125 to 0.125
- tile_mask: int32 [16, 16], replicated, may hold values 0 or 1
Outputs:
- chi: float32 [64, 64], P('aux')
All inputs are finite; a program needn't handle non-finite values.
Results may differ from a plain program's by a relative error of at most 0.0042.
Values may be sent and summed in bfloat16 or wider, within the bound.
A program may use at most 128 MiB of HBM per device.

v0:
```python
import jax
import jax.numpy as jnp
from jax import lax
from jax.sharding import PartitionSpec as P

NAO = 2048
TILE = 128


def swapped(value, axis, apart):
    mask = 2**apart
    pairs = [(source, source ^ mask) for source in range(lax.axis_size(axis))]
    return lax.ppermute(value, axis, pairs)


def shards(coulomb, occupied, virtual, tile_mask):
    rows = lax.axis_size("row")
    cols = lax.axis_size("col")
    pdev, mrow, ncol = coulomb.shape
    nao = mrow * rows
    row_idx = lax.axis_index("row")
    col_idx = lax.axis_index("col")
    aux_idx = lax.axis_index("aux")
    tiles_r = mrow // TILE
    tiles_c = ncol // TILE
    local_tiles = lax.dynamic_slice(
        tile_mask, (row_idx * tiles_r, col_idx * tiles_c), (tiles_r, tiles_c)
    )
    local_mask = jnp.repeat(jnp.repeat(local_tiles, TILE, axis=0), TILE, axis=1).astype(
        jnp.bfloat16
    )
    screened = coulomb * local_mask[None]
    moved = lax.all_to_all(screened, "row", split_axis=0, concat_axis=1, tiled=True)
    pieces = moved.shape[0]
    occ_all, virt_all = (
        lax.all_gather(occupied, "row", axis=0, tiled=True),
        lax.all_gather(virtual, "row", axis=0, tiled=True),
    )
    half = jnp.einsum("ml,pmn->pln", occ_all, moved, preferred_element_type=jnp.float32).astype(
        jnp.bfloat16
    )
    jpart = mrow // cols
    shaped = half.reshape(pieces, rows, cols, jpart, ncol)
    spread = lax.all_to_all(shaped, "col", split_axis=2, concat_axis=4, tiled=True)
    spread = spread.reshape(pieces, rows * jpart, nao)
    dressed = jnp.einsum(
        "pln,ns->pls", spread, virt_all, preferred_element_type=jnp.float32
    ).astype(jnp.bfloat16)
    layered = dressed.reshape(pieces, rows, 1, jpart, cols, ncol)
    returned = lax.all_to_all(
        lax.all_to_all(layered, "row", split_axis=1, concat_axis=0, tiled=True),
        "col",
        split_axis=4,
        concat_axis=2,
        tiled=True,
    )
    aligned = returned.reshape(pdev, mrow, ncol)
    theirs = swapped(screened, "aux", 0)
    with_mine = jnp.einsum("pls,qls->pq", aligned, screened, preferred_element_type=jnp.float32)
    with_theirs = jnp.einsum("pls,qls->pq", aligned, theirs, preferred_element_type=jnp.float32)
    first_half = jnp.where(aux_idx == 0, with_mine, with_theirs)
    second_half = jnp.where(aux_idx == 0, with_theirs, with_mine)
    partial_chi = jnp.concatenate([first_half, second_half], axis=1)
    slots = lax.axis_size("aux")
    placed = jnp.zeros((slots,) + partial_chi.shape, partial_chi.dtype)
    placed = lax.dynamic_update_index_in_dim(placed, partial_chi, aux_idx, 0)
    total = lax.psum(placed, ("aux", "row", "col"))
    total_chi = lax.dynamic_index_in_dim(total, aux_idx, 0, keepdims=False)
    return total_chi / NAO


def solution(mesh):
    placed = (P("aux", "row", "col"), P("row", None), P("row", None), P())
    return jax.shard_map(
        shards, mesh=mesh, in_specs=placed, out_specs=P("aux", None), check_vma=False
    )
```

profile of v0, /device:TPU:1, one launch (start us, length us, event | category | flops | bytes accessed | tf_op | source)
XLA Modules:
  0.0 430.4 jit_solution(17136864265026919637)
XLA Ops:
  6.5 0.0 all-gather.3.cloned.1.call-start
  6.5 0.7 all-gather.3.cloned.1.call-update
  7.3 0.0 all-gather.5.cloned.1.call-start
  7.3 0.7 all-gather.5.cloned.1.call-update
  8.0 0.9 fusion.14
  8.9 0.1 broadcast_bitcast_fusion
  9.0 2.8 copy_multiply_fusion
  11.7 0.8 copy.15
  12.6 79.7 %all_to_all.66 = bf16[32,256,128]{2,1,0:T(8,128)(2,1)} all-to-all(bf16[32,256,128]{2,1,0:T(8,128)(2,1)S(1)} %copy.15), channel_id=1, replica_groups=mesh['aux'=2,'row'=8,'col'=16] {'row'}, dimensions={0} | all-to-all | bytes 4194304 | tf_op jit(solution)/shard_map/all_to_all | solution.py:33
  92.2 4.5 %copy.16 = bf16[8,4,256,128]{2,0,3,1:T(8,128)(2,1)} copy(bf16[8,4,256,128]{3,2,1,0:T(8,128)(2,1)} %bitcast.62) | data formatting | bytes 4194304 | tf_op jit(solution)/shard_map/all_to_all | solution.py:33
  96.7 4.2 all_to_all.51
  100.9 48.7 %all-gather.3.cloned.1.call-done = bf16[2048,2048]{1,0:T(8,128)(2,1)} async-done(((bf16[256,2048]{1,0:T(8,128)(2,1)}), bf16[2048,2048]{1,0:T(8,128)(2,1)}) %all-gather.3.cloned.1.call-update) | async-done | bytes 8388624 | tf_op jit(solution)/shard_map/all_gather | solution.py:36
  149.7 9.8 %fusion.10 = bf16[4,2048,128]{1,2,0:T(8,128)(2,1)} fusion(bf16[4,2048,128]{1,2,0:T(8,128)(2,1)} %all_to_all.51, bf16[2048,2048]{1,0:T(8,128)(2,1)} %all-gather.3.cloned.1.call-done), kind=kOutput, calls=%fused_computation.6 | convolution fusion | flops 4296015872 | bytes 12582912 | tf_op jit(solution)/shard_map/ml,pmn->pln/dot_general | solution.py:39
  159.5 4.0 copy.17
  163.4 2.2 copy.18
  165.6 33.7 %all_to_all.67 = bf16[4,8,16,16,128]{4,3,1,0,2:T(8,128)(2,1)S(1)} all-to-all(bf16[4,8,16,16,128]{4,3,1,0,2:T(8,128)(2,1)S(1)} %copy.18), channel_id=1, replica_groups=mesh['aux'=2,'row'=8,'col'=16] {'col'}, dimensions={2} | all-to-all | bytes 4194304 | tf_op jit(solution)/shard_map/all_to_all | solution.py:44
  199.3 3.7 copy.19
  203.1 4.2 reshape.37
  207.3 37.2 %all-gather.5.cloned.1.call-done = bf16[2048,2048]{1,0:T(8,128)(2,1)} async-done(((bf16[256,2048]{1,0:T(8,128)(2,1)}), bf16[2048,2048]{1,0:T(8,128)(2,1)}) %all-gather.5.cloned.1.call-update) | async-done | bytes 8388624 | tf_op jit(solution)/shard_map/all_gather | solution.py:37
  244.4 8.5 %fusion.7 = bf16[4,128,2048]{2,1,0:T(8,128)(2,1)S(1)} fusion(bf16[4,128,2048]{2,1,0:T(8,128)(2,1)} %reshape.37, bf16[2048,2048]{1,0:T(8,128)(2,1)} %all-gather.5.cloned.1.call-done), kind=kOutput, calls=%fused_computation.5 | convolution fusion | flops 4296015872 | bytes 12582912 | tf_op jit(solution)/shard_map/pln,ns->pls/dot_general | solution.py:46
  253.0 0.6 copy.23
  253.6 0.6 copy.20
  254.2 53.5 %all_to_all.68 = bf16[4,8,1,16,16,128]{5,4,3,0,2,1:T(8,128)(2,1)S(1)} all-to-all(bf16[4,8,1,16,16,128]{5,4,3,0,2,1:T(8,128)(2,1)S(1)} %copy.20), channel_id=1, replica_groups=mesh['aux'=2,'row'=8,'col'=16] {'row'}, dimensions={1} | all-to-all | bytes 4194304 | tf_op jit(solution)/shard_map/all_to_all | solution.py:51
  307.7 1.8 copy.21
  309.6 6.6 %all-to-all-start.3 = ((bf16[32,1,1,16,16,128]{5,3,0,2,1,4:T(8,128)(2,1)}), bf16[32,1,1,16,16,128]{5,3,0,2,1,4:T(8,128)(2,1)}, u32[]{:S(2)}, u32[]{:S(2)}) async-start(bf16[32,1,1,16,16,128]{5,3,0,2,1,4:T(8,128)(2,1)} %copy.21), calls=%async_computation.3 | async-start | bytes 4194304 | tf_op jit(solution)/shard_map/all_to_all | solution.py:50
  316.2 2.8 collective-permute-start
  319.0 22.5 %all-to-all-done.3 = bf16[32,1,1,16,16,128]{5,3,0,2,1,4:T(8,128)(2,1)} async-done(((bf16[32,1,1,16,16,128]{5,3,0,2,1,4:T(8,128)(2,1)}), bf16[32,1,1,16,16,128]{5,3,0,2,1,4:T(8,128)(2,1)}, u32[]{:S(2)}, u32[]{:S(2)}) %all-to-all-start.3) | async-done | bytes 2097184 | tf_op jit(solution)/shard_map/all_to_all | solution.py:50
  341.5 2.1 copy.22
  343.6 0.7 convolution_bitcast_fusion.1
  344.3 0.0 collective-permute-done
  344.3 2.3 broadcast_select_fusion.1
  346.6 0.1 fusion.13
  346.7 76.2 %psum.7 = f32[2,32,64]{2,1,0:T(8,128)S(1)} all-reduce(f32[2,32,64]{2,1,0:T(8,128)S(1)} %fusion.13), channel_id=1, replica_groups=mesh['aux'=2,'row'=8,'col'=16] {'aux','row','col'}, use_global_device_ids=true, to_apply=%region_0.1 | all-reduce | flops 4096 | bytes 32768 | tf_op jit(solution)/shard_map/psum | solution.py:67
  422.9 0.6 multiply_bitcast_fusion
  (1 shorter events, 0.0 us)
Async XLA Ops:
  6.5 143.1 %all-gather.3.cloned.1.call-start = ((), (), s32[]{:S(2)}) async-start(), calls=%async_computation.4 | async-start | bytes 9437184 | tf_op jit(solution)/shard_map/all_gather | solution.py:36
  7.3 237.2 %all-gather.5.cloned.1.call-start = ((), (), s32[]{:S(2)}) async-start(), calls=%async_computation.5 | async-start | bytes 9437184 | tf_op jit(solution)/shard_map/all_gather | solution.py:37
  309.6 31.9 %all-to-all-start.3 = ((bf16[32,1,1,16,16,128]{5,3,0,2,1,4:T(8,128)(2,1)}), bf16[32,1,1,16,16,128]{5,3,0,2,1,4:T(8,128)(2,1)}, u32[]{:S(2)}, u32[]{:S(2)}) async-start(bf16[32,1,1,16,16,128]{5,3,0,2,1,4:T(8,128)(2,1)} %copy.21), calls=%async_computation.3 | async-start | bytes 4194304 | tf_op jit(solution)/shard_map/all_to_all | solution.py:50
  316.2 28.2 %collective-permute-start = (bf16[32,256,128]{2,0,1:T(8,128)(2,1)S(1)}, bf16[32,256,128]{2,0,1:T(8,128)(2,1)}, u32[]{:S(2)}, u32[]{:S(2)}) collective-permute-start(bf16[32,256,128]{2,0,1:T(8,128)(2,1)S(1)} %copy_multiply_fusion), channel_id=1, source_target_pairs={{0,128},{128,0},{1,129},{129,1},{2,130},{130,2},{3,131},{131,3},{4... | collective-permute-start | bytes 6291464 | tf_op jit(solution)/shard_map/ppermute | solution.py:13
Sparse Core Ops, SparseCore 0:
  9.1 140.4 all-gather.2
  151.4 92.9 all-gather.4
where the time goes:
time: 431 us; the launch traced here: 430 us
  blocking collectives  243 us (56%)
  waiting for transfers between devices  110 us (26%)
  local copies, waits for them, and re-layouts  28.9 us (7%)
  matrix products  21.3 us (5%)
  between operations  13.5 us (3%)
  starting transfers between devices  9.44 us (2%)
  other arithmetic  4.33 us (1%)
    all_to_all x1, blocking collectives, shards(): lax.all_to_all(screened, 'row', split_axis=0, concat_axis=1, tiled=True)  79.7 us
    psum x1, blocking collectives, shards(): total = lax.psum(placed, ('aux', 'row', 'col'))  76.2 us
    all_to_all x1, blocking collectives, shards(): lax.all_to_all(layered, 'row', split_axis=1, concat_axis=0, tiled=True)  53.5 us
    all_gather x1, waiting for transfers between devices, shards(): lax.all_gather(occupied, 'row', axis=0, tiled=True)  48.7 us
    all_gather x1, waiting for transfers between devices, shards(): lax.all_gather(virtual, 'row', axis=0, tiled=True)  37.2 us
    all_to_all x1, blocking collectives, shards(): lax.all_to_all(shaped, 'col', split_axis=2, concat_axis=4, tiled=True)  33.7 us
    all_to_all x1, waiting for transfers between devices, shards(): lax.all_to_all(lax.all_to_all(layered, 'row', split_axis=1, concat_axis=0...  22.5 us
    dot_general x1, matrix products, shards(): jnp.einsum('ml,pmn->pln', occ_all, moved, preferred_element_type=jnp.floa...  9.81 us
  transfers between devices with their start and end apart: 4, of which 3 were waited for; matrix products, arithmetic and copies ran while one was open for 8% of the time, Pallas kernels for 0%

commit v1 on v0

--- a/solution.py
+++ b/solution.py
@@ -5,6 +5,39 @@
 
 NAO = 2048
 TILE = 128
+
+
+def _close_modes(s0, dimension_no):
+    mesh_dim = "row"
+    vec_out, x_new, piece_now = (
+        jax.lax.axis_size(mesh_dim),
+        jax.lax.axis_index(mesh_dim),
+        s0.shape[dimension_no],
+    )
+    runs = []
+    for k, w in enumerate(s0.shape):
+        runs.append(w * vec_out if k == dimension_no else w)
+    block_now = lax.dynamic_update_slice_in_dim(
+        jnp.zeros(runs, s0.dtype), s0, x_new * piece_now, axis=dimension_no
+    )
+    main = all_values = s0
+    for dev_i in range(1, vec_out // 2 + 1):
+        pieces_in = []
+        for k in range(vec_out):
+            pieces_in.append((k, (k + 1) % vec_out))
+        main = jax.lax.ppermute(main, mesh_dim, pieces_in)
+        block_now = lax.dynamic_update_slice_in_dim(
+            block_now, main, (x_new - dev_i) % vec_out * piece_now, axis=dimension_no
+        )
+        if 2 * dev_i < vec_out:
+            stack_in = []
+            for k in range(vec_out):
+                stack_in.append((k, (k - 1) % vec_out))
+            all_values = jax.lax.ppermute(all_values, mesh_dim, stack_in)
+            block_now = lax.dynamic_update_slice_in_dim(
+                block_now, all_values, (x_new + dev_i) % vec_out * piece_now, axis=dimension_no
+            )
+    return block_now
 
 
 def swapped(value, axis, apart):
@@ -33,7 +66,7 @@
     moved = lax.all_to_all(screened, "row", split_axis=0, concat_axis=1, tiled=True)
     pieces = moved.shape[0]
     occ_all, virt_all = (
-        lax.all_gather(occupied, "row", axis=0, tiled=True),
+        _close_modes(occupied, 0),
         lax.all_gather(virtual, "row", axis=0, tiled=True),
     )
     half = jnp.einsum("ml,pmn->pln", occ_all, moved, preferred_element_type=jnp.float32).astype(

time: 431 us -> 467 us (1.084)
  blocking collectives: 243 us -> 162 us
  waiting for transfers between devices: 110 us -> 191 us
  local copies, waits for them, and re-layouts: 28.9 us -> 49.4 us
  starting transfers between devices: 9.44 us -> 25.5 us
    ppermute x0 -> x7, waiting for transfers between devices: none -> 172 us  [the longest x3 119 us: _close_modes(): all_values = jax.lax.ppermute(all_values, mesh_dim, stack_in)]
    all_to_all x1 -> x0, blocking collectives: 79.7 us -> none  [shards(): lax.all_to_all(screened, 'row', split_axis=0, concat_axis=1, tiled=True)]
    all_gather x1 -> x0, waiting for transfers between devices: 48.7 us -> none  [shards(): lax.all_gather(occupied, 'row', axis=0, tiled=True)]
    all_gather x1, waiting for transfers between devices: 37.2 us -> 0.01 us  [shards(): lax.all_gather(virtual, 'row', axis=0, tiled=True)]
    dynamic_update_slice x0 -> x8, local copies, waits for them, and re-layouts: none -> 14.9 us  [the longest x4 8.06 us: _close_modes(): lax.dynamic_update_slice_in_dim(block_now, main, (x_new - dev_i) % vec_ou...]
    ppermute x0 -> x7, starting transfers between devices: none -> 8.17 us  [the longest x4 4.22 us: _close_modes(): main = jax.lax.ppermute(main, mesh_dim, pieces_in)]
    all_to_all x0 -> x1, starting transfers between devices: none -> 7.42 us  [shards(): lax.all_to_all(screened, 'row', split_axis=0, concat_axis=1, tiled=True)]
    all_to_all x1, waiting for transfers between devices: 22.5 us -> 17.8 us  [shards(): lax.all_to_all(lax.all_to_all(layered, 'row', split_axis=1, concat_axis=0...]
  transfers between devices with their start and end apart: 4 -> 11, of which waited for: 3 -> 8; matrix products, arithmetic and copies ran while one was open for 8% -> 12% of each run, Pallas kernels for 0% -> 0%
where the time goes in v1:
time: 467 us; the launch traced here: 466 us
  waiting for transfers between devices  191 us (41%)
  blocking collectives  162 us (35%)
  local copies, waits for them, and re-layouts  49.4 us (11%)
  starting transfers between devices  25.5 us (5%)
  matrix products  20.6 us (4%)
  between operations  13.5 us (3%)
    ppermute x3, waiting for transfers between devices, _close_modes(): all_values = jax.lax.ppermute(all_values, mesh_dim, stack_in)  119 us
    psum x1, blocking collectives, shards(): total = lax.psum(placed, ('aux', 'row', 'col'))  78.9 us
    ppermute x4, waiting for transfers between devices, _close_modes(): main = jax.lax.ppermute(main, mesh_dim, pieces_in)  53.6 us
    all_to_all x1, blocking collectives, shards(): lax.all_to_all(layered, 'row', split_axis=1, concat_axis=0, tiled=True)  52 us
    all_to_all x1, blocking collectives, shards(): lax.all_to_all(shaped, 'col', split_axis=2, concat_axis=4, tiled=True)  31.4 us
    all_to_all x1, waiting for transfers between devices, shards(): lax.all_to_all(lax.all_to_all(layered, 'row', split_axis=1, concat_axis=0...  17.8 us
  transfers between devices with their start and end apart: 11, of which 8 were waited for; matrix products, arithmetic and copies ran while one was open for 12% of the time, Pallas kernels for 0%

profile of v1, /device:TPU:1, one launch (start us, length us, event | category | flops | bytes accessed | tf_op | source)
XLA Modules:
  0.0 466.3 jit_solution(642719558786153577)
XLA Ops:
  6.5 0.0 all-gather.2.cloned.1.call-start
  6.5 0.7 all-gather.2.cloned.1.call-update
  7.3 2.5 collective-permute-start
  9.8 0.9 fusion.14
  10.7 0.1 broadcast_bitcast_fusion
  10.7 2.8 copy_multiply_fusion
  13.5 2.1 copy.15
  15.6 0.0 copy-start.1
  15.7 7.4 %all-to-all-start = ((bf16[32,256,128]{2,1,0:T(8,128)(2,1)}), bf16[32,256,128]{2,1,0:T(8,128)(2,1)}, u32[]{:S(2)}, u32[]{:S(2)}) async-start(bf16[32,256,128]{2,1,0:T(8,128)(2,1)} %copy.15), calls=%async_computation | async-start | bytes 4194304 | tf_op jit(solution)/shard_map/all_to_all | solution.py:66
  23.1 0.0 copy-done.1
  23.1 2.7 collective-permute-start.1
  25.7 19.8 %collective-permute-done = bf16[256,2048]{1,0:T(8,128)(2,1)} collective-permute-done((bf16[256,2048]{1,0:T(8,128)(2,1)}, bf16[256,2048]{1,0:T(8,128)(2,1)}, u32[]{:S(2)}, u32[]{:S(2)}) %collective-permute-start) | collective-permute-done | bytes 1048608 | tf_op jit(solution)/shard_map/ppermute | solution.py:28
  45.5 0.0 collective-permute-start.2
  45.5 91.6 %collective-permute-done.1 = bf16[256,2048]{1,0:T(8,128)(2,1)} collective-permute-done((bf16[256,2048]{1,0:T(8,128)(2,1)S(1)}, bf16[256,2048]{1,0:T(8,128)(2,1)}, u32[]{:S(2)}, u32[]{:S(2)}) %collective-permute-start.1) | collective-permute-done | bytes 1048608 | tf_op jit(solution)/shard_map/ppermute | solution.py:36
  137.1 0.0 collective-permute-start.3
  137.1 15.2 %collective-permute-done.2 = bf16[256,2048]{1,0:T(8,128)(2,1)} collective-permute-done((bf16[256,2048]{1,0:T(8,128)(2,1)}, bf16[256,2048]{1,0:T(8,128)(2,1)}, u32[]{:S(2)}, u32[]{:S(2)}) %collective-permute-start.2) | collective-permute-done | bytes 1048608 | tf_op jit(solution)/shard_map/ppermute | solution.py:28
  152.3 1.7 collective-permute-start.4
  153.9 4.3 broadcast_in_dim.17
  158.2 1.1 constant_dynamic-update-slice_fusion.7
  159.4 24.7 %collective-permute-done.3 = bf16[256,2048]{1,0:T(8,128)(2,1)} collective-permute-done((bf16[256,2048]{1,0:T(8,128)(2,1)}, bf16[256,2048]{1,0:T(8,128)(2,1)}, u32[]{:S(2)}, u32[]{:S(2)}) %collective-permute-start.3) | collective-permute-done | bytes 1048608 | tf_op jit(solution)/shard_map/ppermute | solution.py:36
  184.1 1.3 collective-permute-start.5
  185.3 2.3 constant_dynamic-update-slice_fusion.6
  187.7 16.5 %collective-permute-done.4 = bf16[256,2048]{1,0:T(8,128)(2,1)} collective-permute-done((bf16[256,2048]{1,0:T(8,128)(2,1)}, bf16[256,2048]{1,0:T(8,128)(2,1)}, u32[]{:S(2)}, u32[]{:S(2)}) %collective-permute-start.4) | collective-permute-done | bytes 1048608 | tf_op jit(solution)/shard_map/ppermute | solution.py:28
  204.1 0.0 collective-permute-start.6
  204.2 2.3 constant_dynamic-update-slice_fusion.5
  206.4 2.3 constant_dynamic-update-slice_fusion.4
  208.8 2.3 constant_dynamic-update-slice_fusion.3
  211.1 2.3 constant_dynamic-update-slice_fusion.2
  213.4 2.3 collective-permute-done.5
  215.7 1.1 constant_dynamic-update-slice_fusion.1
  216.8 0.0 all-to-all-done
  216.8 4.5 copy.16
  221.3 4.2 all_to_all.51
  225.5 0.0 copy-start
  225.5 2.1 collective-permute-done.6
  227.7 1.1 constant_dynamic-update-slice_fusion
  228.8 0.0 copy-done
  228.8 9.1 %fusion.10 = bf16[4,2048,128]{1,2,0:T(8,128)(2,1)} fusion(bf16[4,2048,128]{1,2,0:T(8,128)(2,1)S(1)} %copy-done, bf16[2048,2048]{1,0:T(8,128)(2,1)} %constant_dynamic-update-slice_fusion), kind=kOutput, calls=%fused_computation.6 | convolution fusion | flops 4296015872 | bytes 12582912 | tf_op jit(solution)/shard_map/ml,pmn->pln/dot_general | solution.py:72
  237.9 3.9 copy.17
  241.9 2.2 copy.18
  244.1 31.4 %all_to_all.66 = bf16[4,8,16,16,128]{4,3,1,0,2:T(8,128)(2,1)S(1)} all-to-all(bf16[4,8,16,16,128]{4,3,1,0,2:T(8,128)(2,1)S(1)} %copy.18), channel_id=1, replica_groups=mesh['aux'=2,'row'=8,'col'=16] {'col'}, dimensions={2} | all-to-all | bytes 4194304 | tf_op jit(solution)/shard_map/all_to_all | solution.py:77
  275.5 3.8 copy.19
  279.2 4.2 reshape.37
  283.4 0.0 all-gather.2.cloned.1.call-done
  283.4 8.5 %fusion.7 = bf16[4,128,2048]{2,1,0:T(8,128)(2,1)S(1)} fusion(bf16[4,128,2048]{2,1,0:T(8,128)(2,1)} %reshape.37, bf16[2048,2048]{1,0:T(8,128)(2,1)} %all-gather.2.cloned.1.call-done), kind=kOutput, calls=%fused_computation.5 | convolution fusion | flops 4296015872 | bytes 12582912 | tf_op jit(solution)/shard_map/pln,ns->pls/dot_general | solution.py:79
  291.9 0.6 copy.23
  292.5 0.6 copy.20
  293.1 52.0 %all_to_all.67 = bf16[4,8,1,16,16,128]{5,4,3,0,2,1:T(8,128)(2,1)S(1)} all-to-all(bf16[4,8,1,16,16,128]{5,4,3,0,2,1:T(8,128)(2,1)S(1)} %copy.20), channel_id=1, replica_groups=mesh['aux'=2,'row'=8,'col'=16] {'row'}, dimensions={1} | all-to-all | bytes 4194304 | tf_op jit(solution)/shard_map/all_to_all | solution.py:84
  345.2 1.9 copy.21
  347.0 4.4 all-to-all-start.3
  351.5 5.5 %collective-permute-start.7 = (bf16[32,256,128]{2,0,1:T(8,128)(2,1)S(1)}, bf16[32,256,128]{2,0,1:T(8,128)(2,1)}, u32[]{:S(2)}, u32[]{:S(2)}) collective-permute-start(bf16[32,256,128]{2,0,1:T(8,128)(2,1)S(1)} %copy_multiply_fusion), channel_id=1, source_target_pairs={{0,128},{128,0},{1,129},{129,1},{2,130},{130,2},{3,131},{131,3},{4... | collective-permute-start | bytes 6291464 | tf_op jit(solution)/shard_map/ppermute | solution.py:46
  357.0 17.8 %all-to-all-done.3 = bf16[32,1,1,16,16,128]{5,3,0,2,1,4:T(8,128)(2,1)} async-done(((bf16[32,1,1,16,16,128]{5,3,0,2,1,4:T(8,128)(2,1)}), bf16[32,1,1,16,16,128]{5,3,0,2,1,4:T(8,128)(2,1)}, u32[]{:S(2)}, u32[]{:S(2)}) %all-to-all-start.3) | async-done | bytes 2097184 | tf_op jit(solution)/shard_map/all_to_all | solution.py:83
  374.7 2.1 copy.22
  376.9 0.7 convolution_bitcast_fusion.1
  377.6 0.0 collective-permute-done.7
  377.6 2.3 broadcast_select_fusion.1
  379.9 0.1 fusion.13
  380.0 78.9 %psum.7 = f32[2,32,64]{2,1,0:T(8,128)S(1)} all-reduce(f32[2,32,64]{2,1,0:T(8,128)S(1)} %fusion.13), channel_id=1, replica_groups=mesh['aux'=2,'row'=8,'col'=16] {'aux','row','col'}, use_global_device_ids=true, to_apply=%region_0.1 | all-reduce | flops 4096 | bytes 32768 | tf_op jit(solution)/shard_map/psum | solution.py:100
  458.8 0.6 multiply_bitcast_fusion
  (1 shorter events, 0.0 us)
Async XLA Ops:
  6.5 276.9 %all-gather.2.cloned.1.call-start = ((), (), s32[]{:S(2)}) async-start(), calls=%async_computation.4 | async-start | bytes 9437184 | tf_op jit(solution)/shard_map/all_gather | solution.py:70
  7.3 38.3 %collective-permute-start = (bf16[256,2048]{1,0:T(8,128)(2,1)}, bf16[256,2048]{1,0:T(8,128)(2,1)}, u32[]{:S(2)}, u32[]{:S(2)}) collective-permute-start(bf16[256,2048]{1,0:T(8,128)(2,1)} %param.5), channel_id=1, source_target_pairs={{0,16},{16,32},{32,48},{48,64},{64,80},{80,96},{96,112},{112,0},{1... | collective-permute-start | bytes 3145736 | tf_op jit(solution)/shard_map/ppermute | solution.py:28
  15.6 7.4 %copy-start.1 = (bf16[256,2048]{1,0:T(8,128)(2,1)S(1)}, bf16[256,2048]{1,0:T(8,128)(2,1)}, u32[]{:S(2)}) copy-start(bf16[256,2048]{1,0:T(8,128)(2,1)} %param.5) | copy-start | bytes 3145732
  15.7 201.2 %all-to-all-start = ((bf16[32,256,128]{2,1,0:T(8,128)(2,1)}), bf16[32,256,128]{2,1,0:T(8,128)(2,1)}, u32[]{:S(2)}, u32[]{:S(2)}) async-start(bf16[32,256,128]{2,1,0:T(8,128)(2,1)} %copy.15), calls=%async_computation | async-start | bytes 4194304 | tf_op jit(solution)/shard_map/all_to_all | solution.py:66
  23.1 114.0 %collective-permute-start.1 = (bf16[256,2048]{1,0:T(8,128)(2,1)S(1)}, bf16[256,2048]{1,0:T(8,128)(2,1)}, u32[]{:S(2)}, u32[]{:S(2)}) collective-permute-start(bf16[256,2048]{1,0:T(8,128)(2,1)S(1)} %copy-done.1), channel_id=1, source_target_pairs={{0,112},{16,0},{32,16},{48,32},{64,48},{80,64},{96,80},{112,96},{1... | collective-permute-start | bytes 3145736 | tf_op jit(solution)/shard_map/ppermute | solution.py:36
  45.5 106.7 %collective-permute-start.2 = (bf16[256,2048]{1,0:T(8,128)(2,1)}, bf16[256,2048]{1,0:T(8,128)(2,1)}, u32[]{:S(2)}, u32[]{:S(2)}) collective-permute-start(bf16[256,2048]{1,0:T(8,128)(2,1)} %collective-permute-done), channel_id=1, source_target_pairs={{0,16},{16,32},{32,48},{48,64},{64,80},{80,96},{96,112},{112,0},{1... | collective-permute-start | bytes 3145736 | tf_op jit(solution)/shard_map/ppermute | solution.py:28
  137.1 47.0 %collective-permute-start.3 = (bf16[256,2048]{1,0:T(8,128)(2,1)}, bf16[256,2048]{1,0:T(8,128)(2,1)}, u32[]{:S(2)}, u32[]{:S(2)}) collective-permute-start(bf16[256,2048]{1,0:T(8,128)(2,1)} %collective-permute-done.1), channel_id=1, source_target_pairs={{0,112},{16,0},{32,16},{48,32},{64,48},{80,64},{96,80},{112,96},{1... | collective-permute-start | bytes 3145736 | tf_op jit(solution)/shard_map/ppermute | solution.py:36
  152.3 51.9 %collective-permute-start.4 = (bf16[256,2048]{1,0:T(8,128)(2,1)}, bf16[256,2048]{1,0:T(8,128)(2,1)}, u32[]{:S(2)}, u32[]{:S(2)}) collective-permute-start(bf16[256,2048]{1,0:T(8,128)(2,1)} %collective-permute-done.2), channel_id=1, source_target_pairs={{0,16},{16,32},{32,48},{48,64},{64,80},{80,96},{96,112},{112,0},{1... | collective-permute-start | bytes 3145736 | tf_op jit(solution)/shard_map/ppermute | solution.py:28
  184.1 31.7 %collective-permute-start.5 = (bf16[256,2048]{1,0:T(8,128)(2,1)}, bf16[256,2048]{1,0:T(8,128)(2,1)S(1)}, u32[]{:S(2)}, u32[]{:S(2)}) collective-permute-start(bf16[256,2048]{1,0:T(8,128)(2,1)} %collective-permute-done.3), channel_id=1, source_target_pairs={{0,112},{16,0},{32,16},{48,32},{64,48},{80,64},{96,80},{112,96},{1... | collective-permute-start | bytes 3145736 | tf_op jit(solution)/shard_map/ppermute | solution.py:36
  204.1 23.5 %collective-permute-start.6 = (bf16[256,2048]{1,0:T(8,128)(2,1)}, bf16[256,2048]{1,0:T(8,128)(2,1)S(1)}, u32[]{:S(2)}, u32[]{:S(2)}) collective-permute-start(bf16[256,2048]{1,0:T(8,128)(2,1)} %collective-permute-done.4), channel_id=1, source_target_pairs={{0,16},{16,32},{32,48},{48,64},{64,80},{80,96},{96,112},{112,0},{1... | collective-permute-start | bytes 3145736 | tf_op jit(solution)/shard_map/ppermute | solution.py:28
  225.5 3.3 copy-start
  347.0 27.7 %all-to-all-start.3 = ((bf16[32,1,1,16,16,128]{5,3,0,2,1,4:T(8,128)(2,1)}), bf16[32,1,1,16,16,128]{5,3,0,2,1,4:T(8,128)(2,1)}, u32[]{:S(2)}, u32[]{:S(2)}) async-start(bf16[32,1,1,16,16,128]{5,3,0,2,1,4:T(8,128)(2,1)} %copy.21), calls=%async_computation.3 | async-start | bytes 4194304 | tf_op jit(solution)/shard_map/all_to_all | solution.py:83
  351.5 26.1 %collective-permute-start.7 = (bf16[32,256,128]{2,0,1:T(8,128)(2,1)S(1)}, bf16[32,256,128]{2,0,1:T(8,128)(2,1)}, u32[]{:S(2)}, u32[]{:S(2)}) collective-permute-start(bf16[32,256,128]{2,0,1:T(8,128)(2,1)S(1)} %copy_multiply_fusion), channel_id=1, source_target_pairs={{0,128},{128,0},{1,129},{129,1},{2,130},{130,2},{3,131},{131,3},{4... | collective-permute-start | bytes 6291464 | tf_op jit(solution)/shard_map/ppermute | solution.py:46
Sparse Core Ops, SparseCore 0:
  9.1 196.5 all-gather.1
